TPU v7x, 32 devices: a whole 2x2x4 slice. The times are simulated.
32 devices in a mesh: row: 4 (over y, x), col: 8 (over z, core).
Axes of the slice: x: 2, y: 2, z: 4, core: 2. Of those that a mesh axis runs over, the one named last changes fastest.
Arguments:
- parent_entries: float32 [16384, 16384], P('row', 'col'), may hold values from -1.5 to 1.5
- children: float32 [6144, 12288], P('row', 'col'), may hold values from -1.5 to 1.5
- shift: float32 [16384], P('row'), may hold values from 24 to 48
- child_map: int32 [2, 96], replicated, may hold values from 0 to 255, as said below
Outputs:
- factored_front: float32 [16384, 16384], P('row', 'col')
Inputs may be any that keep to these rules, and one draw needn't show every extreme that they name: `child_map`: row k sends child k's tiles to distinct parent tiles. For each child and each residue s modulo 4, the entries at positions congruent to s hold at most 8 values of any one residue modulo 4 and at most 8 of any one residue modulo 8, both bounds reached for every s; for each residue v modulo 4, exactly 24 entries of a row are congruent to v.
All inputs are finite; a program needn't handle non-finite values.
Results may differ from a plain program's by a relative error of at most 0.00005.
Values sent between devices are 32-bit elements; how exact they have to be, the bound alone decides.
A program may use at most 448 MiB of HBM per device.

v0:
```python
import jax
import jax.numpy as jnp
from jax import lax
from jax.sharding import PartitionSpec as P

TILE = 64


def from_root(value, axis, source):
    kept = jnp.where(lax.axis_index(axis) == source, value, 0).astype(value.dtype)
    return lax.psum(kept, axis)


def outgoing(block_map, sources, grid_size, own_index, slot_count):
    groups = block_map.shape[0] // sources
    block_table = jnp.take(block_map.reshape(groups, sources), own_index, axis=1)
    target = block_table % grid_size
    ordinal = jnp.arange(groups)
    earlier = (target[:, None] == target[None, :]) & (ordinal[None, :] < ordinal[:, None])
    earlier_count = jnp.sum(earlier.astype(jnp.int32), axis=1)
    picked = (target[None, :, None] == jnp.arange(grid_size)[:, None, None]) & (
        earlier_count[None, :, None] == jnp.arange(slot_count)[None, None, :]
    )
    return jnp.sum(jnp.where(picked, ordinal[None, :, None], 0), axis=1)


def incoming(block_map, sources, grid_size, own_index, slot_count):
    groups = block_map.shape[0] // sources
    block_table = block_map.reshape(groups, sources).T
    to_here = block_table % grid_size == own_index
    counts = to_here.astype(jnp.int32)
    earlier_count = jnp.cumsum(counts, axis=1) - counts
    picked = to_here[:, :, None] & (
        earlier_count[:, :, None] == jnp.arange(slot_count)[None, None, :]
    )
    present = jnp.any(picked, axis=1)
    target = jnp.sum(jnp.where(picked, block_table[:, :, None], 0), axis=1)
    return (present, target)


def compacted(block_map, grid_size, own_index, slot_count, groups):
    present, target = incoming(block_map, grid_size, grid_size, own_index, slot_count)
    flat_present = present.reshape(-1)
    flat_target = target.reshape(-1)
    counts = flat_present.astype(jnp.int32)
    position = jnp.cumsum(counts) - counts
    picked = flat_present[None, :] & (position[None, :] == jnp.arange(groups)[:, None])
    chosen = jnp.sum(jnp.where(picked, jnp.arange(flat_present.shape[0])[None, :], 0), axis=1)
    blocks = jnp.sum(jnp.where(picked, flat_target[None, :], 0), axis=1)
    return (chosen, blocks)


def local(parent_entries, children, shift, child_map):
    rows_here, cols_here = parent_entries.shape
    grid_rows = lax.axis_size("row")
    grid_cols = lax.axis_size("col")
    half_grid = grid_cols // 2
    row_index = lax.axis_index("row")
    col_index = lax.axis_index("col")
    child_now = col_index // half_grid
    half_col = col_index % half_grid
    child_width = children.shape[1]
    groups = children.shape[0] // TILE
    col_groups = child_width // TILE
    slot_count = groups // grid_rows + 2
    own_map = jnp.take(child_map, child_now, axis=0)
    row_blocks = rows_here // TILE
    col_blocks = cols_here // TILE
    col_present = []
    col_targets = []
    for child in range(2):
        present, target = incoming(child_map[child], half_grid, grid_cols, col_index, slot_count)
        col_present.append(present)
        col_targets.append(target)
    col_local = jnp.where(
        jnp.concatenate(col_present, axis=0),
        jnp.concatenate(col_targets, axis=0) // grid_cols,
        col_blocks,
    )
    front_tiles = parent_entries.reshape(row_blocks, TILE, col_blocks, TILE)
    chosen_lists = []
    row_lists = []
    for child in range(2):
        chosen, blocks = compacted(child_map[child], grid_rows, row_index, slot_count, groups)
        chosen_lists.append(chosen)
        row_lists.append(blocks)
    own_chosen = jnp.take(jnp.stack(chosen_lists), child_now, axis=0)
    first_sources = outgoing(own_map, grid_rows, grid_rows, row_index, slot_count)
    child_blocks = children.reshape(groups, TILE, child_width)
    outbound = jnp.take(child_blocks, first_sources.reshape(-1), axis=0).reshape(
        grid_rows, slot_count, TILE, child_width
    )
    arrived = lax.all_to_all(outbound, "row", split_axis=0, concat_axis=0, tiled=True)
    gathered_rows = jnp.take(
        arrived.reshape(grid_rows * slot_count, TILE, child_width), own_chosen, axis=0
    )
    second_sources = outgoing(own_map, half_grid, grid_cols, half_col, slot_count)
    child_tiles = jnp.moveaxis(gathered_rows.reshape(groups, TILE, col_groups, TILE), 2, 0)
    outbound_tiles = jnp.take(child_tiles, second_sources.reshape(-1), axis=0).reshape(
        grid_cols, slot_count, groups, TILE * TILE
    )
    arrived_tiles = lax.all_to_all(outbound_tiles, "col", split_axis=0, concat_axis=0, tiled=True)
    row_local = jnp.repeat(jnp.stack(row_lists), half_grid, axis=0) // grid_rows
    updates = arrived_tiles.reshape(grid_cols, slot_count, groups, TILE, TILE)
    front_tiles = front_tiles.at[row_local[:, None, :], :, col_local[:, :, None], :].add(
        updates, mode="drop"
    )
    row_global = jnp.arange(row_blocks) * grid_rows + row_index
    col_global = jnp.arange(col_blocks) * grid_cols + col_index
    diagonal_tile = row_global[:, None] == col_global[None, :]
    identity = jnp.eye(TILE, dtype=bool)
    shift_tiles = shift.reshape(row_blocks, TILE)
    front_tiles = front_tiles + jnp.where(
        diagonal_tile[:, None, :, None] & identity[None, :, None, :],
        shift_tiles[:, :, None, None],
        0.0,
    )
    parent_front_matrix = front_tiles.reshape(rows_here, cols_here)
    eliminated = TILE * grid_cols
    corner = parent_front_matrix[: 2 * TILE, :TILE].reshape(1, 2 * TILE * TILE)
    corners = lax.all_gather(corner, ("row", "col"), axis=0, tiled=True)
    leading_block = (
        corners.reshape(grid_rows, grid_cols, 2, TILE, TILE)
        .transpose(2, 0, 3, 1, 4)
        .reshape(eliminated, eliminated)
    )
    pivot_block = jnp.linalg.cholesky((leading_block + leading_block.T) * 0.5)
    panel_t = parent_front_matrix[:, :TILE].T
    gathered = lax.all_gather(panel_t, "col", axis=0, tiled=True)
    factor_t = jax.scipy.linalg.solve_triangular(pivot_block, gathered, lower=True)
    own_pivot = jnp.concatenate(
        [
            lax.dynamic_slice_in_dim(pivot_block, row_index * TILE, TILE, 0),
            lax.dynamic_slice_in_dim(pivot_block, (row_index + grid_rows) * TILE, TILE, 0),
        ],
        axis=0,
    )
    factor_t = factor_t.at[:, : 2 * TILE].set(own_pivot.T)
    parity = col_index // grid_rows
    halves = factor_t.reshape(eliminated, row_blocks // 2, 2, TILE)
    picked = lax.dynamic_index_in_dim(halves, parity, axis=2, keepdims=False).reshape(
        eliminated, cols_here
    )
    col_factor = from_root(picked, "row", col_index % grid_rows)
    update = lax.dot_general(
        factor_t,
        col_factor,
        (((0,), (0,)), ((), ())),
        precision=lax.Precision.HIGHEST,
        preferred_element_type=jnp.float32,
    )
    result = parent_front_matrix - update
    panel_out = lax.dynamic_slice_in_dim(factor_t, col_index * TILE, TILE, 0).T
    result = result.at[:, :TILE].set(panel_out)
    result = result.at[: 2 * TILE, TILE:].set(0.0)
    return result


def solution(mesh):
    in_specs = (P("row", "col"), P("row", "col"), P("row"), P())
    out_specs = P("row", "col")
    return jax.shard_map(local, mesh=mesh, in_specs=in_specs, out_specs=out_specs, check_vma=False)
```

profile of v0, /device:TPU:0, one launch (start us, length us, event | category | flops | bytes accessed | tf_op | source)
XLA Modules:
  0.0 1655.5 jit_solution(12107706643401894546)
XLA Ops:
  17.9 11.8 broadcast_select_fusion.1
  39.8 135.1 %all-to-all-done = f32[4,8,64,1536]{3,2,1,0:T(8,128)} async-done(((f32[4,8,64,1536]{3,2,1,0:T(8,128)}), f32[4,8,64,1536]{3,2,1,0:T(8,128)}, u32[]{:S(2)}, u32[]{:S(2)}) %all-to-all-start) | async-done | bytes 12582944 | tf_op jit(solution)/shard_map/all_to_all | solution.py:93
  184.2 14.5 gather.37
  198.7 15.7 fusion
  214.5 30.4 %gather_fusion.2 = f32[64,24,64,64]{3,2,1,0:T(8,128)} fusion(f32[24,24,64,64]{3,2,1,0:T(8,128)} %fusion, s32[1024]{0:T(1024)S(1)} %pad_clamp_fusion), kind=kCustom, calls=%fused_computation.2 | custom fusion | bytes 50331904 | tf_op jit(solution)/shard_map/jit(_take)/gather | solution.py:99
  244.9 40.7 %gather.39 = f32[8,8,24,4096]{3,2,1,0:T(8,128)} reshape(f32[64,24,64,64]{3,2,1,0:T(8,128)} %gather_fusion.2) | data formatting | bytes 50331648 | tf_op jit(solution)/shard_map/jit(_take)/gather | solution.py:99
  285.5 17.8 %broadcast_select_fusion = f32[8,8,24,4096]{3,2,1,0:T(8,128)} fusion(f32[8,8,24,4096]{3,2,1,0:T(8,128)} %gather.39, pred[8,8]{1,0:T(8,128)(4,1)S(1)} %compare_and_fusion), kind=kLoop, calls=%fused_computation.10 | loop fusion | flops 6291456 | bytes 50331712 | tf_op jit(solution)/shard_map/jit(_take)/select_n | solution.py:99
  310.0 54.2 %reshape.592 = f32[64,64,32,64]{3,2,1,0:T(8,128)} reshape(f32[4096,2048]{1,0:T(8,128)} %param.12) | data formatting | bytes 67108864 | tf_op jit(solution)/shard_map/reshape | solution.py:80
  365.2 66.1 %copy_add_fusion = f32[64,64,32,64]{3,1,2,0:T(8,128)} fusion(f32[64,64,32,64]{3,2,1,0:T(8,128)} %reshape.592, f32[64,64]{1,0:T(8,128)S(1)} %broadcast_in_dim.220, pred[64,64]{1,0:T(8,128)(4,1)S(1)} %iota_compare_fusion.3, pred[64,32]{1,0:T(8,128)(4,1)S(1)} %broadcast_compare_fusion), kind=kLoop, calls=%fused_computation.6 | loop fusion | flops 25165824 | bytes 67131392 | tf_op jit(solution)/shard_map/add.94
  431.3 421.9 %all-to-all-done.1 = f32[8,8,24,4096]{3,2,1,0:T(8,128)} async-done(((f32[8,8,24,4096]{3,2,1,0:T(8,128)}), f32[8,8,24,4096]{3,2,1,0:T(8,128)}, u32[]{:S(2)}, u32[]{:S(2)}) %all-to-all-start.1) | async-done | bytes 25165856 | tf_op jit(solution)/shard_map/all_to_all | solution.py:102
  853.2 39.6 %reshape.767 = f32[1536,64,64]{2,1,0:T(8,128)} reshape(f32[8,8,24,4096]{3,2,1,0:T(8,128)} %all-to-all-done.1) | data formatting | bytes 50331648 | tf_op jit(solution)/shard_map/reshape | solution.py:104
  892.8 211.3 %scatter_fusion = f32[2048,64,64]{2,1,0:T(8,128)} fusion(f32[2048,64,64]{2,1,0:T(8,128)} %bitcast.1, s32[1536]{0:T(1024)S(1)} %reshape.765, f32[1536,64,64]{2,1,0:T(8,128)} %reshape.767), kind=kCustom, calls=%fused_computation.3 | custom fusion | flops 6291456 | bytes 75503616
  1104.1 56.3 %copy.70 = f32[64,64,32,64]{3,2,1,0:T(8,128)} copy(f32[64,64,32,64]{3,1,2,0:T(8,128)} %bitcast.19) | data formatting | bytes 67108864 | tf_op jit(solution)/shard_map/scatter-add | solution.py:105
  1160.4 56.4 %reshape.601 = f32[4096,2048]{1,0:T(8,128)} reshape(f32[64,64,32,64]{3,2,1,0:T(8,128)} %copy.70) | data formatting | bytes 67108864 | tf_op jit(solution)/shard_map/reshape | solution.py:118
  1222.5 47.0 %all-gather.6.cloned.1.call-done = f32[32,1,8192]{2,1,0:T(1,128)} async-done(((f32[1,1,8192]{2,1,0:T(1,128)}), f32[32,1,8192]{2,1,0:T(1,128)}) %all-gather.6.cloned.1.call-update) | async-done | bytes 1048592 | tf_op jit(solution)/shard_map/all_gather | solution.py:121
  1280.5 11.7 cholesky.104
  1302.8 11.7 cholesky.217
  1314.6 10.0 custom-call.32
  1325.2 11.7 cholesky.238
  1347.4 11.9 cholesky.255
  1372.1 39.9 %custom-call.34 = f32[4,128,128]{1,2,0:T(8,128)} custom-call(f32[4,128,128]{2,1,0:T(8,128)S(1)} %get-tuple-element.73), custom_call_target="InvertDiagBlocksLowerTriangular" | custom-call | tf_op jit(solution)/shard_map/jit(_solve_triangular)/triangular_solve | solution.py:130
  1459.9 101.6 %all-reduce.3.cloned.1.call-done = f32[512,2048]{0,1:T(8,128)} async-done(((f32[512,2048]{0,1:T(8,128)}), f32[512,2048]{0,1:T(8,128)}) %all-reduce.3.cloned.1.call-update) | async-done | bytes 4194320 | tf_op jit(solution)/shard_map/psum | solution.py:11
  1561.5 61.7 %convolution_subtract_fusion = f32[4096,2048]{1,0:T(8,128)} fusion(f32[4096,2048]{1,0:T(8,128)} %reshape.601, f32[512,4096]{0,1:T(8,128)} %copy-done, f32[512,2048]{0,1:T(8,128)} %all-reduce.3.cloned.1.call-done), kind=kOutput, calls=%fused_computation.9 | convolution fusion | flops 51547996160 | bytes 79691776 | tf_op jit(solution)/shard_map/dot_general | solution.py:145
  1626.6 10.4 scatter.11
  (171 shorter events, 157.3 us)
Async XLA Ops:
  29.8 145.1 %all-to-all-start = ((f32[4,8,64,1536]{3,2,1,0:T(8,128)}), f32[4,8,64,1536]{3,2,1,0:T(8,128)}, u32[]{:S(2)}, u32[]{:S(2)}) async-start(f32[4,8,64,1536]{3,2,1,0:T(8,128)} %broadcast_select_fusion.1), calls=%async_computation | async-start | bytes 25165824 | tf_op jit(solution)/shard_map/all_to_all | solution.py:93
  303.3 549.9 %all-to-all-start.1 = ((f32[8,8,24,4096]{3,2,1,0:T(8,128)}), f32[8,8,24,4096]{3,2,1,0:T(8,128)}, u32[]{:S(2)}, u32[]{:S(2)}) async-start(f32[8,8,24,4096]{3,2,1,0:T(8,128)} %broadcast_select_fusion), calls=%async_computation.1 | async-start | bytes 50331648 | tf_op jit(solution)/shard_map/all_to_all | solution.py:102
  309.8 54.5 %copy-start.4 = (f32[4096]{0:T(1024)S(1)}, f32[4096]{0:T(1024)}, u32[]{:S(2)}) copy-start(f32[4096]{0:T(1024)} %param.14) | copy-start | bytes 49156
  309.8 55.0 %copy-start.6 = (s32[2]{0:T(128)S(1)}, s32[2]{0:T(128)}, u32[]{:S(2)}) copy-start(s32[2]{0:T(128)} %constant.427) | copy-start | bytes 28
  309.8 55.1 %copy-start.5 = (s32[2]{0:T(128)S(1)}, s32[2]{0:T(128)}, u32[]{:S(2)}) copy-start(s32[2]{0:T(128)} %constant.430) | copy-start | bytes 28
  309.8 959.7 %all-gather.6.cloned.1.call-start = ((), (), s32[]{:S(2)}) async-start(), calls=%async_computation.4 | async-start | bytes 1081344 | tf_op jit(solution)/shard_map/all_gather | solution.py:121
  1218.4 193.6 %all-gather.4.cloned.1.call-start = ((), (), s32[]{:S(2)}) async-start(), calls=%async_computation.2 | async-start | bytes 9437184 | tf_op jit(solution)/shard_map/all_gather | solution.py:129
  1221.8 339.7 %all-reduce.3.cloned.1.call-start = ((), (), s32[]{:S(2)}) async-start(), calls=%async_computation.3 | async-start | bytes 8388608 | tf_op jit(solution)/shard_map/psum | solution.py:11
  1440.0 11.2 copy-start.1
  1440.0 11.2 copy-start.2
  1440.0 11.2 copy-start.3
  1452.0 7.2 copy-start.7
  1452.7 3.2 copy-start
Sparse Core Ops, SparseCore 0:
  1218.6 50.9 all-gather.5
  1271.1 81.0 all-gather.3
  1458.8 102.6 all-reduce.2
where the time goes:
time: 1670 us; the launch traced here: 1660 us
  waiting for transfers between devices  706 us (42%)
  other arithmetic  463 us (28%)
  local copies, waits for them, and re-layouts  362 us (22%)
  matrix products  94.6 us (6%)
    all_to_all x1, waiting for transfers between devices, local(): lax.all_to_all(outbound_tiles, 'col', split_axis=0, concat_axis=0, tiled=...  422 us
    unnamed x5, other arithmetic  212 us
    all_to_all x1, waiting for transfers between devices, local(): lax.all_to_all(outbound, 'row', split_axis=0, concat_axis=0, tiled=True)  135 us
    psum x1, waiting for transfers between devices, from_root(): return lax.psum(kept, axis)  102 us
    another operation x15, other arithmetic, local(): pivot_block = jnp.linalg.cholesky((leading_block + leading_block.T) * 0.5)  79.2 us
    another operation x10, other arithmetic  74.7 us
    gather x2, local copies, waits for them, and re-layouts, local(): jnp.take(child_tiles, second_sources.reshape(-1), axis=0)  71.1 us
    dot_general x1, matrix products, local(): lax.dot_general(factor_t, col_factor, (((0,), (0,)), ((), ())), precision...  61.7 us
  transfers between devices with their start and end apart: 5, of which 4 were waited for; matrix products, arithmetic and copies ran while one was open for 16% of the time, Pallas kernels for 0%

commit v1 on v0

--- a/solution.py
+++ b/solution.py
@@ -8,7 +8,7 @@
 
 def from_root(value, axis, source):
     kept = jnp.where(lax.axis_index(axis) == source, value, 0).astype(value.dtype)
-    return lax.psum(kept, axis)
+    return jnp.sum(lax.all_gather(kept, axis), axis=0)
 
 
 def outgoing(block_map, sources, grid_size, own_index, slot_count):

time: 1670 us -> 1750 us (1.048)
  waiting for transfers between devices: 706 us -> 759 us
    all_gather x0 -> x1, waiting for transfers between devices: none -> 155 us  [from_root(): return jnp.sum(lax.all_gather(kept, axis), axis=0)]
    psum x1 -> x0, waiting for transfers between devices: 102 us -> none  [from_root(): return lax.psum(kept, axis)]
    unnamed x5 -> x6, other arithmetic: 212 us -> 222 us
where the time goes in v1:
time: 1750 us; the launch traced here: 1730 us
  waiting for transfers between devices  759 us (43%)
  other arithmetic  474 us (27%)
  local copies, waits for them, and re-layouts  376 us (21%)
  matrix products  94.6 us (5%)
    all_to_all x1, waiting for transfers between devices, local(): lax.all_to_all(outbound_tiles, 'col', split_axis=0, concat_axis=0, tiled=...  422 us
    unnamed x6, other arithmetic  222 us
    all_gather x1, waiting for transfers between devices, from_root(): return jnp.sum(lax.all_gather(kept, axis), axis=0)  155 us
    all_to_all x1, waiting for transfers between devices, local(): lax.all_to_all(outbound, 'row', split_axis=0, concat_axis=0, tiled=True)  135 us
    another operation x15, other arithmetic, local(): pivot_block = jnp.linalg.cholesky((leading_block + leading_block.T) * 0.5)  79.5 us
    another operation x10, other arithmetic  74.9 us
    gather x2, local copies, waits for them, and re-layouts, local(): jnp.take(child_tiles, second_sources.reshape(-1), axis=0)  71.1 us
    dot_general x1, matrix products, local(): lax.dot_general(factor_t, col_factor, (((0,), (0,)), ((), ())), precision...  61.6 us
  transfers between devices with their start and end apart: 5, of which 4 were waited for; matrix products, arithmetic and copies ran while one was open for 16% of the time, Pallas kernels for 0%

profile of v1, /device:TPU:0, one launch (start us, length us, event | category | flops | bytes accessed | tf_op | source)
XLA Modules:
  0.0 1733.3 jit_solution(14786046561488728825)
XLA Ops:
  17.9 11.8 broadcast_select_fusion.1
  39.8 135.1 %all-to-all-done = f32[4,8,64,1536]{3,2,1,0:T(8,128)} async-done(((f32[4,8,64,1536]{3,2,1,0:T(8,128)}), f32[4,8,64,1536]{3,2,1,0:T(8,128)}, u32[]{:S(2)}, u32[]{:S(2)}) %all-to-all-start) | async-done | bytes 12582944 | tf_op jit(solution)/shard_map/all_to_all | solution.py:93
  184.2 14.5 gather.37
  198.7 15.7 fusion
  214.5 30.4 %gather_fusion.2 = f32[64,24,64,64]{3,2,1,0:T(8,128)} fusion(f32[24,24,64,64]{3,2,1,0:T(8,128)} %fusion, s32[1024]{0:T(1024)S(1)} %pad_clamp_fusion), kind=kCustom, calls=%fused_computation.2 | custom fusion | bytes 50331904 | tf_op jit(solution)/shard_map/jit(_take)/gather | solution.py:99
  244.9 40.7 %gather.39 = f32[8,8,24,4096]{3,2,1,0:T(8,128)} reshape(f32[64,24,64,64]{3,2,1,0:T(8,128)} %gather_fusion.2) | data formatting | bytes 50331648 | tf_op jit(solution)/shard_map/jit(_take)/gather | solution.py:99
  285.5 17.8 %broadcast_select_fusion = f32[8,8,24,4096]{3,2,1,0:T(8,128)} fusion(f32[8,8,24,4096]{3,2,1,0:T(8,128)} %gather.39, pred[8,8]{1,0:T(8,128)(4,1)S(1)} %compare_and_fusion), kind=kLoop, calls=%fused_computation.10 | loop fusion | flops 6291456 | bytes 50331712 | tf_op jit(solution)/shard_map/jit(_take)/select_n | solution.py:99
  310.1 54.2 %reshape.602 = f32[64,64,32,64]{3,2,1,0:T(8,128)} reshape(f32[4096,2048]{1,0:T(8,128)} %param.12) | data formatting | bytes 67108864 | tf_op jit(solution)/shard_map/reshape | solution.py:80
  365.2 66.1 %copy_add_fusion = f32[64,64,32,64]{3,1,2,0:T(8,128)} fusion(f32[64,64,32,64]{3,2,1,0:T(8,128)} %reshape.602, f32[64,64]{1,0:T(8,128)S(1)} %broadcast_in_dim.220, pred[64,64]{1,0:T(8,128)(4,1)S(1)} %iota_compare_fusion.3, pred[64,32]{1,0:T(8,128)(4,1)S(1)} %broadcast_compare_fusion), kind=kLoop, calls=%fused_computation.6 | loop fusion | flops 25165824 | bytes 67131392 | tf_op jit(solution)/shard_map/add.93
  431.4 421.8 %all-to-all-done.1 = f32[8,8,24,4096]{3,2,1,0:T(8,128)} async-done(((f32[8,8,24,4096]{3,2,1,0:T(8,128)}), f32[8,8,24,4096]{3,2,1,0:T(8,128)}, u32[]{:S(2)}, u32[]{:S(2)}) %all-to-all-start.1) | async-done | bytes 25165856 | tf_op jit(solution)/shard_map/all_to_all | solution.py:102
  853.2 39.6 %reshape.777 = f32[1536,64,64]{2,1,0:T(8,128)} reshape(f32[8,8,24,4096]{3,2,1,0:T(8,128)} %all-to-all-done.1) | data formatting | bytes 50331648 | tf_op jit(solution)/shard_map/reshape | solution.py:104
  892.8 211.3 %scatter_fusion = f32[2048,64,64]{2,1,0:T(8,128)} fusion(f32[2048,64,64]{2,1,0:T(8,128)} %bitcast.1, s32[1536]{0:T(1024)S(1)} %reshape.775, f32[1536,64,64]{2,1,0:T(8,128)} %reshape.777), kind=kCustom, calls=%fused_computation.3 | custom fusion | flops 6291456 | bytes 75503616
  1104.1 56.3 %copy.91 = f32[64,64,32,64]{3,2,1,0:T(8,128)} copy(f32[64,64,32,64]{3,1,2,0:T(8,128)} %bitcast.19) | data formatting | bytes 67108864 | tf_op jit(solution)/shard_map/scatter-add | solution.py:105
  1160.4 56.4 %reshape.611 = f32[4096,2048]{1,0:T(8,128)} reshape(f32[64,64,32,64]{3,2,1,0:T(8,128)} %copy.91) | data formatting | bytes 67108864 | tf_op jit(solution)/shard_map/reshape | solution.py:118
  1222.5 47.0 %all-gather.9.cloned.1.call-done = f32[32,1,8192]{2,1,0:T(1,128)} async-done(((f32[1,1,8192]{2,1,0:T(1,128)}), f32[32,1,8192]{2,1,0:T(1,128)}) %all-gather.9.cloned.1.call-update) | async-done | bytes 1048592 | tf_op jit(solution)/shard_map/all_gather | solution.py:121
  1276.1 11.6 reshape.614
  1288.8 11.7 cholesky.104
  1311.2 11.7 cholesky.217
  1333.6 11.7 cholesky.238
  1355.8 12.1 cholesky.255
  1380.7 39.9 %custom-call.34 = f32[4,128,128]{1,2,0:T(8,128)} custom-call(f32[4,128,128]{2,1,0:T(8,128)S(1)} %get-tuple-element.73), custom_call_target="InvertDiagBlocksLowerTriangular" | custom-call | tf_op jit(solution)/shard_map/jit(_solve_triangular)/triangular_solve | solution.py:130
  1473.8 155.0 %all-gather.7.cloned.1.call-done = f32[4,512,2048]{2,1,0:T(8,128)} async-done(((f32[1,512,2048]{2,1,0:T(8,128)}), f32[4,512,2048]{2,1,0:T(8,128)}) %all-gather.7.cloned.1.call-update) | async-done | bytes 16777232 | tf_op jit(solution)/shard_map/all_gather | solution.py:11
  1639.0 61.6 %convolution_subtract_fusion = f32[4096,2048]{1,0:T(8,128)} fusion(f32[4096,2048]{1,0:T(8,128)} %reshape.611, f32[512,4096]{0,1:T(8,128)} %copy-done, f32[512,2048]{1,0:T(8,128)} %reduce_sum.129), kind=kOutput, calls=%fused_computation.9 | convolution fusion | flops 51547996160 | bytes 79691776 | tf_op jit(solution)/shard_map/dot_general | solution.py:145
  1704.1 10.4 scatter.11
  (173 shorter events, 179.7 us)
Async XLA Ops:
  29.8 145.1 %all-to-all-start = ((f32[4,8,64,1536]{3,2,1,0:T(8,128)}), f32[4,8,64,1536]{3,2,1,0:T(8,128)}, u32[]{:S(2)}, u32[]{:S(2)}) async-start(f32[4,8,64,1536]{3,2,1,0:T(8,128)} %broadcast_select_fusion.1), calls=%async_computation | async-start | bytes 25165824 | tf_op jit(solution)/shard_map/all_to_all | solution.py:93
  303.3 549.9 %all-to-all-start.1 = ((f32[8,8,24,4096]{3,2,1,0:T(8,128)}), f32[8,8,24,4096]{3,2,1,0:T(8,128)}, u32[]{:S(2)}, u32[]{:S(2)}) async-start(f32[8,8,24,4096]{3,2,1,0:T(8,128)} %broadcast_select_fusion), calls=%async_computation.1 | async-start | bytes 50331648 | tf_op jit(solution)/shard_map/all_to_all | solution.py:102
  309.8 54.6 %copy-start.4 = (f32[4096]{0:T(1024)S(1)}, f32[4096]{0:T(1024)}, u32[]{:S(2)}) copy-start(f32[4096]{0:T(1024)} %param.14) | copy-start | bytes 49156
  309.8 55.1 %copy-start.6 = (s32[2]{0:T(128)S(1)}, s32[2]{0:T(128)}, u32[]{:S(2)}) copy-start(s32[2]{0:T(128)} %constant.427) | copy-start | bytes 28
  309.8 55.1 %copy-start.5 = (s32[2]{0:T(128)S(1)}, s32[2]{0:T(128)}, u32[]{:S(2)}) copy-start(s32[2]{0:T(128)} %constant.430) | copy-start | bytes 28
  309.8 959.7 %all-gather.9.cloned.1.call-start = ((), (), s32[]{:S(2)}) async-start(), calls=%async_computation.4 | async-start | bytes 1081344 | tf_op jit(solution)/shard_map/all_gather | solution.py:121
  1218.4 202.2 %all-gather.5.cloned.1.call-start = ((), (), s32[]{:S(2)}) async-start(), calls=%async_computation.2 | async-start | bytes 9437184 | tf_op jit(solution)/shard_map/all_gather | solution.py:129
  1221.8 407.0 %all-gather.7.cloned.1.call-start = ((), (), s32[]{:S(2)}) async-start(), calls=%async_computation.3 | async-start | bytes 20971520 | tf_op jit(solution)/shard_map/all_gather | solution.py:11
  1448.4 11.2 copy-start.1
  1448.4 11.2 copy-start.2
  1448.4 11.2 copy-start.3
  1461.1 3.2 copy-start
  1466.9 6.1 copy-start.7
Sparse Core Ops, SparseCore 0:
  1218.6 50.9 all-gather.8
  1271.1 81.0 all-gather.4
  1472.5 156.2 all-gather.6
